TPU v7x, 32 devices: a whole 2x2x4 slice. The times are simulated.
32 devices in a mesh: depth: 2 (over core), row: 4 (over y, x), col: 4 (over z).
Axes of the slice: x: 2, y: 2, z: 4, core: 2. Of those that a mesh axis runs over, the one named last changes fastest.
Arguments:
- tile_left: bfloat16 [16, 16, 64, 1024], P('row', 'col'), may hold values from -6 to 6
- tile_right: bfloat16 [16, 16, 64, 1024], P('row', 'col'), may hold values from -6 to 6
- row_left: bfloat16 [16, 8, 64, 1024], P('row', 'depth', None, 'col'), may hold values from -6 to 6
- row_right: bfloat16 [16, 8, 64, 1024], P('row', 'depth', None, 'col'), may hold values from -0.1875 to 0.1875
- col_left: bfloat16 [16, 8, 64, 1024], P('col', 'depth', None, 'row'), may hold values from -6 to 6
- col_right: bfloat16 [16, 8, 64, 1024], P('col', 'depth', None, 'row'), may hold values from -0.1875 to 0.1875
- row_mask: int32 [16, 8], P('row', 'depth'), may hold values 0 or 1
- col_mask: int32 [16, 8], P('col', 'depth'), may hold values 0 or 1
- sketch: bfloat16 [64, 1024], replicated, may hold values from -1 to 1
Outputs:
- new_left: float32 [16, 16, 64, 1024], P('row', 'col', 'depth')
- new_right: float32 [16, 16, 64, 1024], P('row', 'col', 'depth')
All inputs are finite; a program needn't handle non-finite values. No bound on the sum of `row_mask` or of `col_mask` on one device may be relied on, other than what follows from the above.
Results may differ from a plain program's by a relative error of at most 0.0003.
Values may be sent and summed in bfloat16 or wider, within the bound.
No kernel may reach another device: no remote copies, remote signals or barrier semaphores. Data moves between devices by JAX's collectives and lax.ppermute only.
A program may use at most 64 MiB of HBM per device.

v0:
```python
import math
import jax
import jax.numpy as jnp
from jax import lax
from jax.sharding import PartitionSpec as P

NB = 1024
K = 64
exact_mode = lax.Precision.HIGHEST


def orthonormalize(sketched):
    for repeat in range(2):
        gram_mat = jnp.einsum("ijtn,ijsn->ijts", sketched, sketched, precision=exact_mode)
        factor = jnp.linalg.cholesky(gram_mat)
        sketched = jax.scipy.linalg.solve_triangular(factor, sketched, lower=True)
    return sketched


def on_device(
    tile_left, tile_right, row_left, row_right, col_left, col_right, row_mask, col_mask, sketch
):
    row_full_left, row_full_right = (
        lax.all_gather(row_left, "col", axis=3, tiled=True),
        lax.all_gather(row_right, "col", axis=3, tiled=True),
    )
    col_full_left, col_full_right = (
        lax.all_gather(col_left, "row", axis=3, tiled=True),
        lax.all_gather(col_right, "row", axis=3, tiled=True),
    )
    weight_table = (
        row_mask.astype(jnp.float32)[:, None, :] * col_mask.astype(jnp.float32)[None, :, :]
    )
    coupling = jnp.einsum(
        "ikrn,jksn->ijkrs", row_full_right, col_full_right, preferred_element_type=jnp.float32
    )
    coupling = coupling * weight_table[:, :, :, None, None]
    col_sketch = jnp.einsum(
        "jksn,tn->jkst", col_full_left, sketch, preferred_element_type=jnp.float32
    )
    mixing = jnp.einsum("ijkrs,jkst->ijkrt", coupling, col_sketch, precision=exact_mode)
    partial_sketch = -jnp.einsum(
        "ijkrt,ikrn->ijtn",
        mixing,
        row_full_left,
        precision=exact_mode,
        preferred_element_type=jnp.float32,
    )
    sketch_right = jnp.einsum(
        "ijrn,tn->ijrt", tile_right, sketch, preferred_element_type=jnp.float32
    )
    summed = lax.psum(partial_sketch, "depth")
    sketched = summed + jnp.einsum(
        "ijrt,ijrn->ijtn",
        sketch_right,
        tile_left,
        precision=exact_mode,
        preferred_element_type=jnp.float32,
    )
    basis = orthonormalize(sketched)
    rank_rows = K // lax.axis_size("depth")
    rank_offset = lax.axis_index("depth") * rank_rows
    basis_mine = lax.dynamic_slice_in_dim(basis, rank_offset, rank_rows, 2)
    basis_row = jnp.einsum(
        "ijtn,ikrn->ijktr",
        basis,
        row_full_left,
        precision=exact_mode,
        preferred_element_type=jnp.float32,
    )
    projected = jnp.einsum("ijktr,ijkrs->ijkts", basis_row, coupling, precision=exact_mode)
    right_part = -jnp.einsum(
        "ijkts,jksn->ijtn",
        projected,
        col_full_left,
        precision=exact_mode,
        preferred_element_type=jnp.float32,
    )
    right_share = lax.psum_scatter(right_part, "depth", scatter_dimension=2, tiled=True)
    own_part = jnp.einsum(
        "ijtn,ijrn->ijtr",
        basis_mine,
        tile_left,
        precision=exact_mode,
        preferred_element_type=jnp.float32,
    )
    right_share = right_share + jnp.einsum(
        "ijtr,ijrn->ijtn",
        own_part,
        tile_right,
        precision=exact_mode,
        preferred_element_type=jnp.float32,
    )
    return (basis_mine * math.sqrt(NB), right_share / math.sqrt(NB))


def solution(mesh):
    in_specs = (
        P("row", "col", None, None),
        P("row", "col", None, None),
        P("row", "depth", None, "col"),
        P("row", "depth", None, "col"),
        P("col", "depth", None, "row"),
        P("col", "depth", None, "row"),
        P("row", "depth"),
        P("col", "depth"),
        P(),
    )
    out_specs = (P("row", "col", "depth", None), P("row", "col", "depth", None))
    return jax.shard_map(
        on_device, mesh=mesh, in_specs=in_specs, out_specs=out_specs, check_vma=False
    )
```

profile of v0, /device:TPU:0, one launch (start us, length us, event | category | flops | bytes accessed | tf_op | source)
XLA Modules:
  0.0 626.7 jit_solution(12347719536717495241)
XLA Ops:
  7.2 0.0 copy-start
  7.2 0.0 all-gather.5.cloned.1.call-start
  7.3 0.7 all-gather.5.cloned.1.call-update
  8.0 0.0 all-gather.7.cloned.1.call-start
  8.0 1.9 copy.21
  9.9 0.0 all-gather.7.cloned.1.call-update
  9.9 0.0 all-gather.9.cloned.1.call-start
  10.0 0.8 copy.22
  10.8 0.0 all-gather.9.cloned.1.call-update
  10.8 0.0 all-gather.11.cloned.1.call-start
  10.9 0.5 all-gather.11.cloned.1.call-update
  11.4 0.0 all-reduce.2.cloned.1.call-start
  11.5 0.1 copy.23
  11.6 0.1 copy.24
  11.7 0.1 broadcast_multiply_fusion
  11.8 35.9 %all-gather.5.cloned.1.call-done = bf16[4,4,64,1024]{3,2,1,0:T(8,128)(2,1)} async-done(((bf16[4,4,64,256]{3,2,1,0:T(8,128)(2,1)}), bf16[4,4,64,1024]{3,2,1,0:T(8,128)(2,1)}) %all-gather.5.cloned.1.call-update) | async-done | bytes 2097168 | tf_op jit(solution)/shard_map/all_gather | solution.py:28
  47.7 0.0 copy-done.10
  47.7 2.3 convolution_bitcast_fusion
  49.9 35.2 %all-gather.7.cloned.1.call-done = bf16[4,4,64,1024]{3,2,0,1:T(8,128)(2,1)} async-done(((bf16[4,4,64,256]{3,2,0,1:T(8,128)(2,1)}), bf16[4,4,64,1024]{3,2,0,1:T(8,128)(2,1)}) %all-gather.7.cloned.1.call-update) | async-done | bytes 2097168 | tf_op jit(solution)/shard_map/all_gather | solution.py:29
  85.1 48.4 %all-gather.9.cloned.1.call-done = bf16[4,4,64,1024]{3,2,0,1:T(8,128)(2,1)} async-done(((bf16[4,4,64,256]{3,2,0,1:T(8,128)(2,1)}), bf16[4,4,64,1024]{3,2,0,1:T(8,128)(2,1)}) %all-gather.9.cloned.1.call-update) | async-done | bytes 2097168 | tf_op jit(solution)/shard_map/all_gather | solution.py:25
  133.6 3.5 bitcast_multiply_fusion
  137.1 0.0 copy-start.6
  137.1 1.3 copy-done.6
  138.4 3.3 fusion.15
  141.7 37.8 %all-gather.11.cloned.1.call-done = bf16[4,4,64,1024]{3,2,1,0:T(8,128)(2,1)} async-done(((bf16[4,4,64,256]{3,2,1,0:T(8,128)(2,1)}), bf16[4,4,64,1024]{3,2,1,0:T(8,128)(2,1)}) %all-gather.11.cloned.1.call-update) | async-done | bytes 2097168 | tf_op jit(solution)/shard_map/all_gather | solution.py:24
  179.5 6.2 bitcast_negate_fusion.1
  185.6 0.0 all-reduce.2.cloned.1.call-update
  185.6 0.3 reduce-scatter.2.cloned.1.call-start
  186.0 2.7 fusion.32
  188.7 23.4 %all-reduce.2.cloned.1.call-done = f32[4,4,64,1024]{3,2,1,0:T(8,128)} async-done(((f32[4,4,64,1024]{3,2,1,0:T(8,128)}), f32[4,4,64,1024]{3,2,1,0:T(8,128)}) %all-reduce.2.cloned.1.call-update) | async-done | bytes 4194320 | tf_op jit(solution)/shard_map/psum | solution.py:52
  212.1 4.1 convolution_add_fusion
  216.2 1.9 copy-done.2
  218.2 4.0 fusion.36
  222.2 0.2 copy.25
  222.4 0.9 fusion.30
  223.3 95.0 %custom-call.8 = f32[4,4,64,64]{3,2,1,0:T(8,128)S(1)} custom-call(f32[4,4,64,64]{3,2,1,0:T(8,128)} %fusion.30), custom_call_target="Cholesky" | custom-call | tf_op jit(solution)/shard_map/jit(cholesky)/cholesky | solution.py:15
  318.3 0.1 select_reduce_fusion.1
  318.3 0.1 compare_reduce_fusion.1
  318.5 0.1 select_bitcast_fusion.1
  318.6 78.6 %custom-call.9 = f32[4,4,1,64,64]{3,4,2,1,0:T(8,128)S(1)} custom-call(f32[4,4,1,64,64]{4,3,2,1,0:T(8,128)S(1)} %select_bitcast_fusion.1), custom_call_target="InvertDiagBlocksLowerTriangular" | custom-call | tf_op jit(solution)/shard_map/jit(_solve_triangular)/vmap(vmap())/triangular_solve | solution.py:16
  397.3 5.5 fusion.28
  402.8 1.9 copy-done.1
  404.7 4.0 fusion.37
  408.8 0.2 copy.27
  409.0 0.9 fusion.27
  409.8 94.5 %custom-call.10 = f32[4,4,64,64]{3,2,1,0:T(8,128)S(1)} custom-call(f32[4,4,64,64]{3,2,1,0:T(8,128)} %fusion.27), custom_call_target="Cholesky" | custom-call | tf_op jit(solution)/shard_map/jit(cholesky)/cholesky | solution.py:15
  504.3 0.1 select_reduce_fusion
  504.4 0.1 compare_reduce_fusion
  504.6 0.1 select_bitcast_fusion
  504.7 78.6 %custom-call.11 = f32[4,4,1,64,64]{3,4,2,1,0:T(8,128)S(1)} custom-call(f32[4,4,1,64,64]{4,3,2,1,0:T(8,128)S(1)} %select_bitcast_fusion), custom_call_target="InvertDiagBlocksLowerTriangular" | custom-call | tf_op jit(solution)/shard_map/jit(_solve_triangular)/vmap(vmap())/triangular_solve | solution.py:16
  583.3 0.0 copy-start.5
  583.4 5.8 fusion.25
  589.2 3.5 fusion
  592.6 0.0 copy-start.7
  592.7 1.4 copy.61
  594.1 0.2 copy-done.7
  594.2 3.5 fusion.12
  597.8 3.7 fusion.2
  601.4 0.0 reduce-scatter.2.cloned.1.call-update
  601.5 3.4 dynamic-slice_multiply_fusion
  604.9 1.8 fusion.17
  606.7 8.1 %reduce-scatter.2.cloned.1.call-done = f32[4,4,32,1024]{3,2,0,1:T(8,128)} async-done(((f32[4,4,64,1024]{3,2,0,1:T(8,128)}), f32[4,4,32,1024]{3,2,0,1:T(8,128)}) %reduce-scatter.2.cloned.1.call-update) | async-done | bytes 2097168 | tf_op jit(solution)/shard_map/reduce_scatter | solution.py:79
  614.8 3.3 add_multiply_fusion
  618.2 1.5 copy.30
  (21 shorter events, 0.1 us)
Async XLA Ops:
  7.2 204.9 %copy-start = (bf16[4,4,64,1024]{3,2,1,0:T(8,128)(2,1)S(1)}, bf16[4,4,64,1024]{3,2,1,0:T(8,128)(2,1)}, u32[]{:S(2)}) copy-start(bf16[4,4,64,1024]{3,2,1,0:T(8,128)(2,1)} %param.12) | copy-start | bytes 6291460
  7.2 2.8 copy-start.9
  7.2 4.3 copy-start.11
  7.2 4.4 copy-start.12
  7.2 40.4 %copy-start.10 = (bf16[64,1024]{1,0:T(8,128)(2,1)S(1)}, bf16[64,1024]{1,0:T(8,128)(2,1)}, u32[]{:S(2)}) copy-start(bf16[64,1024]{1,0:T(8,128)(2,1)} %param.20) | copy-start | bytes 393220
  7.2 40.4 %all-gather.5.cloned.1.call-start = ((), (), s32[]{:S(2)}) async-start(), calls=%async_computation.1 | async-start | bytes 2621440 | tf_op jit(solution)/shard_map/all_gather | solution.py:28
  8.0 77.2 %all-gather.7.cloned.1.call-start = ((), (), s32[]{:S(2)}) async-start(), calls=%async_computation.2 | async-start | bytes 2621440 | tf_op jit(solution)/shard_map/all_gather | solution.py:29
  9.9 123.6 %all-gather.9.cloned.1.call-start = ((), (), s32[]{:S(2)}) async-start(), calls=%async_computation.3 | async-start | bytes 2621440 | tf_op jit(solution)/shard_map/all_gather | solution.py:25
  10.8 168.6 %all-gather.11.cloned.1.call-start = ((), (), s32[]{:S(2)}) async-start(), calls=%async_computation.4 | async-start | bytes 2621440 | tf_op jit(solution)/shard_map/all_gather | solution.py:24
  11.4 200.7 %all-reduce.2.cloned.1.call-start = ((), (), s32[]{:S(2)}) async-start(), calls=%async_computation.5 | async-start | bytes 8388608 | tf_op jit(solution)/shard_map/psum | solution.py:52
  137.1 1.3 copy-start.6
  185.6 429.2 %reduce-scatter.2.cloned.1.call-start = ((), (), s32[]{:S(2)}) async-start(), calls=%async_computation.6 | async-start | bytes 6291456 | tf_op jit(solution)/shard_map/reduce_scatter | solution.py:79
  216.2 1.9 copy-start.2
  402.8 1.9 copy-start.1
  583.3 5.8 copy-start.5
  589.2 3.5 copy-start.3
  592.6 1.6 copy-start.7
  594.2 3.5 copy-start.8
  601.5 3.4 copy-start.4
Sparse Core Ops, SparseCore 0:
  9.9 37.7 all-gather.4
  50.1 35.0 all-gather.6
  87.3 46.2 all-gather.8
  135.0 44.4 all-gather.10
  185.8 26.2 all-reduce.1
  601.6 13.2 reduce-scatter.1
where the time goes:
time: 632 us; the launch traced here: 627 us
  other arithmetic  353 us (56%)
  waiting for transfers between devices  190 us (30%)
  matrix products  57.2 us (9%)
  between operations  14.6 us (2%)
  local copies, waits for them, and re-layouts  11.6 us (2%)
    another operation x7, other arithmetic, orthonormalize(): factor = jnp.linalg.cholesky(gram_mat)  190 us
    another operation x5, other arithmetic, orthonormalize(): sketched = jax.scipy.linalg.solve_triangular(factor, sketched, lower=True)  158 us
    all_gather x1, waiting for transfers between devices, on_device(): lax.all_gather(row_right, 'col', axis=3, tiled=True)  48.4 us
    all_gather x1, waiting for transfers between devices, on_device(): lax.all_gather(row_left, 'col', axis=3, tiled=True)  37.8 us
    all_gather x1, waiting for transfers between devices, on_device(): lax.all_gather(col_left, 'row', axis=3, tiled=True)  35.9 us
    all_gather x1, waiting for transfers between devices, on_device(): lax.all_gather(col_right, 'row', axis=3, tiled=True)  35.2 us
    psum x1, waiting for transfers between devices, on_device(): summed = lax.psum(partial_sketch, 'depth')  23.4 us
  transfers between devices with their start and end apart: 6, of which 6 were waited for; matrix products, arithmetic and copies ran while one was open for 3% of the time, Pallas kernels for 0%

commit v1 on v0

--- a/solution.py
+++ b/solution.py
@@ -7,6 +7,19 @@
 NB = 1024
 K = 64
 exact_mode = lax.Precision.HIGHEST
+
+
+def collect(value, axis, dim):
+    ways = lax.axis_size(axis)
+    up = [(d, (d + 1) % ways) for d in range(ways)]
+    down = [(d, (d - 1) % ways) for d in range(ways)]
+    earlier, later = ([value], [value])
+    for _ in range(ways // 2):
+        earlier.append(lax.ppermute(earlier[-1], axis, up))
+    for _ in range((ways - 1) // 2):
+        later.append(lax.ppermute(later[-1], axis, down))
+    line = jnp.concatenate([*earlier[::-1], *later[1:]], axis=dim)
+    return jnp.roll(line, (lax.axis_index(axis) - ways // 2) * value.shape[dim], axis=dim)
 
 
 def orthonormalize(sketched):
@@ -25,7 +38,7 @@
         lax.all_gather(row_right, "col", axis=3, tiled=True),
     )
     col_full_left, col_full_right = (
-        lax.all_gather(col_left, "row", axis=3, tiled=True),
+        collect(col_left, "row", 3),
         lax.all_gather(col_right, "row", axis=3, tiled=True),
     )
     weight_table = (

time: 632 us -> 611 us (0.967)
  waiting for transfers between devices: 190 us -> 155 us
  local copies, waits for them, and re-layouts: 11.6 us -> 19.5 us
    ppermute x0 -> x3, waiting for transfers between devices: none -> 48.5 us  [the longest x2 35.9 us: collect(): earlier.append(lax.ppermute(earlier[-1], axis, up))]
    all_gather x1 -> x0, waiting for transfers between devices: 35.9 us -> none  [on_device(): lax.all_gather(col_left, 'row', axis=3, tiled=True)]
    all_gather x1, waiting for transfers between devices: 35.2 us -> 0.02 us  [on_device(): lax.all_gather(col_right, 'row', axis=3, tiled=True)]
    all_gather x1, waiting for transfers between devices: 48.4 us -> 38.2 us  [on_device(): lax.all_gather(row_right, 'col', axis=3, tiled=True)]
    unnamed x29 -> x40, local copies, waits for them, and re-layouts: 9.61 us -> 16.4 us
  transfers between devices with their start and end apart: 6 -> 8, of which waited for: 6 -> 7; matrix products, arithmetic and copies ran while one was open for 3% -> 4% of each run, Pallas kernels for 0% -> 0%
where the time goes in v1:
time: 611 us; the launch traced here: 605 us
  other arithmetic  355 us (58%)
  waiting for transfers between devices  155 us (25%)
  matrix products  54.6 us (9%)
  local copies, waits for them, and re-layouts  19.5 us (3%)
  between operations  14.4 us (2%)
  starting transfers between devices  6.55 us (1%)
    another operation x7, other arithmetic, orthonormalize(): factor = jnp.linalg.cholesky(gram_mat)  190 us
    another operation x5, other arithmetic, orthonormalize(): sketched = jax.scipy.linalg.solve_triangular(factor, sketched, lower=True)  158 us
    all_gather x1, waiting for transfers between devices, on_device(): lax.all_gather(row_right, 'col', axis=3, tiled=True)  38.2 us
    all_gather x1, waiting for transfers between devices, on_device(): lax.all_gather(row_left, 'col', axis=3, tiled=True)  37.9 us
    ppermute x2, waiting for transfers between devices, collect(): earlier.append(lax.ppermute(earlier[-1], axis, up))  35.9 us
    psum x1, waiting for transfers between devices, on_device(): summed = lax.psum(partial_sketch, 'depth')  23.4 us
    unnamed x40, local copies, waits for them, and re-layouts  16.4 us
    ppermute x1, waiting for transfers between devices, collect(): later.append(lax.ppermute(later[-1], axis, down))  12.6 us
  transfers between devices with their start and end apart: 8, of which 7 were waited for; matrix products, arithmetic and copies ran while one was open for 4% of the time, Pallas kernels for 0%

profile of v1, /device:TPU:0, one launch (start us, length us, event | category | flops | bytes accessed | tf_op | source)
XLA Modules:
  0.0 604.9 jit_solution(13630602385648024625)
XLA Ops:
  7.3 2.0 copy.21
  9.3 0.0 all-gather.6.cloned.1.call-start
  9.4 1.9 copy.22
  11.3 0.7 all-gather.8.cloned.1.call-update
  12.1 3.0 collective-permute-start
  15.1 17.4 %collective-permute-done = bf16[4,4,64,256]{3,2,1,0:T(8,128)(2,1)S(1)} collective-permute-done((bf16[4,4,64,256]{3,2,1,0:T(8,128)(2,1)S(1)}, bf16[4,4,64,256]{3,2,1,0:T(8,128)(2,1)S(1)}, u32[]{:S(2)}, u32[]{:S(2)}) %collective-permute-start) | collective-permute-done | bytes 524320 | tf_op jit(solution)/shard_map/ppermute | solution.py:18
  32.5 1.9 collective-permute-start.1
  34.4 1.1 collective-permute-start.2
  35.5 0.1 copy.23
  35.6 0.1 copy.24
  35.7 0.1 broadcast_multiply_fusion
  35.8 18.5 %collective-permute-done.1 = bf16[4,4,64,256]{3,2,1,0:T(8,128)(2,1)} collective-permute-done((bf16[4,4,64,256]{3,2,1,0:T(8,128)(2,1)S(1)}, bf16[4,4,64,256]{3,2,1,0:T(8,128)(2,1)}, u32[]{:S(2)}, u32[]{:S(2)}) %collective-permute-start.1) | collective-permute-done | bytes 524320 | tf_op jit(solution)/shard_map/ppermute | solution.py:18
  54.3 1.1 constant_dynamic-update-slice_fusion.7
  55.5 0.1 constant_dynamic-update-slice_fusion.6
  55.5 0.1 constant_dynamic-update-slice_fusion.5
  55.6 12.6 %collective-permute-done.2 = bf16[4,4,64,256]{3,2,1,0:T(8,128)(2,1)} collective-permute-done((bf16[4,4,64,256]{3,2,1,0:T(8,128)(2,1)S(1)}, bf16[4,4,64,256]{3,2,1,0:T(8,128)(2,1)}, u32[]{:S(2)}, u32[]{:S(2)}) %collective-permute-start.2) | collective-permute-done | bytes 524320 | tf_op jit(solution)/shard_map/ppermute | solution.py:20
  68.2 1.1 constant_dynamic-update-slice_fusion.4
  69.3 1.1 constant_dynamic-update-slice_fusion.3
  70.4 0.1 constant_dynamic-update-slice_fusion.2
  70.5 0.1 constant_dynamic-update-slice_fusion.1
  70.6 1.1 constant_dynamic-update-slice_fusion
  71.7 1.9 copy-done.9
  73.7 0.7 fusion.26
  74.4 38.2 %all-gather.6.cloned.1.call-done = bf16[4,4,64,1024]{3,2,0,1:T(8,128)(2,1)} async-done(((bf16[4,4,64,256]{3,2,0,1:T(8,128)(2,1)}), bf16[4,4,64,1024]{3,2,0,1:T(8,128)(2,1)}) %all-gather.6.cloned.1.call-update) | async-done | bytes 2097168 | tf_op jit(solution)/shard_map/all_gather | solution.py:38
  112.6 3.5 bitcast_multiply_fusion
  116.1 1.3 copy-done.6
  117.4 3.3 fusion.15
  120.7 37.9 %all-gather.8.cloned.1.call-done = bf16[4,4,64,1024]{3,2,1,0:T(8,128)(2,1)} async-done(((bf16[4,4,64,256]{3,2,1,0:T(8,128)(2,1)}), bf16[4,4,64,1024]{3,2,1,0:T(8,128)(2,1)}) %all-gather.8.cloned.1.call-update) | async-done | bytes 2097168 | tf_op jit(solution)/shard_map/all_gather | solution.py:37
  158.6 6.2 %bitcast_negate_fusion.1 = f32[4,4,64,1024]{3,2,1,0:T(8,128)} fusion(bf16[4,4,64,1024]{3,2,1,0:T(8,128)(2,1)} %all-gather.8.cloned.1.call-done, f32[4,4,64,4,64]{4,2,1,0,3:T(8,128)} %fusion.15), kind=kOutput, calls=%fused_computation.4 | convolution fusion | flops 3222274048 | bytes 7340032 | tf_op jit(solution)/shard_map/ijkrt,ikrn->ijtn/dot_general | solution.py:55
  164.8 0.3 reduce-scatter.2.cloned.1.call-start
  165.2 2.7 fusion.36
  167.9 23.4 %all-reduce.2.cloned.1.call-done = f32[4,4,64,1024]{3,2,1,0:T(8,128)} async-done(((f32[4,4,64,1024]{3,2,1,0:T(8,128)}), f32[4,4,64,1024]{3,2,1,0:T(8,128)}) %all-reduce.2.cloned.1.call-update) | async-done | bytes 4194320 | tf_op jit(solution)/shard_map/psum | solution.py:65
  191.3 4.1 convolution_add_fusion
  195.4 2.0 copy-done.2
  197.4 4.0 fusion.42
  201.4 0.2 copy.25
  201.6 0.9 fusion.34
  202.5 95.0 %custom-call.8 = f32[4,4,64,64]{3,2,1,0:T(8,128)S(1)} custom-call(f32[4,4,64,64]{3,2,1,0:T(8,128)} %fusion.34), custom_call_target="Cholesky" | custom-call | tf_op jit(solution)/shard_map/jit(cholesky)/cholesky | solution.py:28
  297.5 0.1 select_reduce_fusion.1
  297.6 0.1 compare_reduce_fusion.1
  297.7 0.1 select_bitcast_fusion.1
  297.8 78.6 %custom-call.9 = f32[4,4,1,64,64]{3,4,2,1,0:T(8,128)S(1)} custom-call(f32[4,4,1,64,64]{4,3,2,1,0:T(8,128)S(1)} %select_bitcast_fusion.1), custom_call_target="InvertDiagBlocksLowerTriangular" | custom-call | tf_op jit(solution)/shard_map/jit(_solve_triangular)/vmap(vmap())/triangular_solve | solution.py:29
  376.5 5.5 fusion.32
  382.0 2.0 copy-done.1
  384.0 4.0 fusion.43
  388.0 0.2 copy.27
  388.2 0.9 fusion.31
  389.1 94.5 %custom-call.10 = f32[4,4,64,64]{3,2,1,0:T(8,128)S(1)} custom-call(f32[4,4,64,64]{3,2,1,0:T(8,128)} %fusion.31), custom_call_target="Cholesky" | custom-call | tf_op jit(solution)/shard_map/jit(cholesky)/cholesky | solution.py:28
  483.6 0.1 select_reduce_fusion
  483.6 0.1 compare_reduce_fusion
  483.8 0.1 select_bitcast_fusion
  483.9 78.6 %custom-call.11 = f32[4,4,1,64,64]{3,4,2,1,0:T(8,128)S(1)} custom-call(f32[4,4,1,64,64]{4,3,2,1,0:T(8,128)S(1)} %select_bitcast_fusion), custom_call_target="InvertDiagBlocksLowerTriangular" | custom-call | tf_op jit(solution)/shard_map/jit(_solve_triangular)/vmap(vmap())/triangular_solve | solution.py:29
  562.6 5.8 fusion.29
  568.4 3.5 fusion
  571.9 1.4 copy.59
  573.3 0.2 copy-done.7
  573.5 3.5 fusion.12
  577.0 3.7 fusion.2
  580.7 3.4 dynamic-slice_multiply_fusion
  584.1 1.8 fusion.17
  585.9 2.3 fusion.10
  588.2 5.8 reduce-scatter.2.cloned.1.call-done
  594.1 2.6 add_multiply_fusion
  596.7 1.5 copy.30
  (37 shorter events, 0.3 us)
Async XLA Ops:
  7.2 184.1 %copy-start = (bf16[4,4,64,1024]{3,2,1,0:T(8,128)(2,1)S(1)}, bf16[4,4,64,1024]{3,2,1,0:T(8,128)(2,1)}, u32[]{:S(2)}) copy-start(bf16[4,4,64,1024]{3,2,1,0:T(8,128)(2,1)} %param.12) | copy-start | bytes 6291460
  7.2 4.9 copy-start.11
  7.2 28.3 %copy-start.13 = (s32[4,4]{1,0:T(4,128)S(1)}, s32[4,4]{1,0:T(4,128)}, u32[]{:S(2)}) copy-start(s32[4,4]{1,0:T(4,128)} %param.18) | copy-start | bytes 196
  7.2 28.4 %copy-start.14 = (s32[4,4]{1,0:T(4,128)S(1)}, s32[4,4]{1,0:T(4,128)}, u32[]{:S(2)}) copy-start(s32[4,4]{1,0:T(4,128)} %param.19) | copy-start | bytes 196
  7.2 67.2 %all-gather.4.cloned.1.call-start = ((), (), s32[]{:S(2)}) async-start(), calls=%async_computation.1 | async-start | bytes 2621440 | tf_op jit(solution)/shard_map/all_gather | solution.py:42
  9.3 103.3 %all-gather.6.cloned.1.call-start = ((), (), s32[]{:S(2)}) async-start(), calls=%async_computation.2 | async-start | bytes 2621440 | tf_op jit(solution)/shard_map/all_gather | solution.py:38
  11.3 147.4 %all-gather.8.cloned.1.call-start = ((), (), s32[]{:S(2)}) async-start(), calls=%async_computation.3 | async-start | bytes 2621440 | tf_op jit(solution)/shard_map/all_gather | solution.py:37
  12.0 179.3 %all-reduce.2.cloned.1.call-start = ((), (), s32[]{:S(2)}) async-start(), calls=%async_computation.4 | async-start | bytes 8388608 | tf_op jit(solution)/shard_map/psum | solution.py:65
  12.1 20.4 %collective-permute-start = (bf16[4,4,64,256]{3,2,1,0:T(8,128)(2,1)S(1)}, bf16[4,4,64,256]{3,2,1,0:T(8,128)(2,1)S(1)}, u32[]{:S(2)}, u32[]{:S(2)}) collective-permute-start(bf16[4,4,64,256]{3,2,1,0:T(8,128)(2,1)S(1)} %copy-done.11), channel_id=1, source_target_pairs={{0,4},{4,8},{8,12},{12,0},{1,5},{5,9},{9,13},{13,1},{2,6},{6,10},{... | collective-permute-start | bytes 1572872 | tf_op jit(solution)/shard_map/ppermute | solution.py:18
  32.5 21.9 %collective-permute-start.1 = (bf16[4,4,64,256]{3,2,1,0:T(8,128)(2,1)S(1)}, bf16[4,4,64,256]{3,2,1,0:T(8,128)(2,1)}, u32[]{:S(2)}, u32[]{:S(2)}) collective-permute-start(bf16[4,4,64,256]{3,2,1,0:T(8,128)(2,1)S(1)} %collective-permute-done), channel_id=1, source_target_pairs={{0,4},{4,8},{8,12},{12,0},{1,5},{5,9},{9,13},{13,1},{2,6},{6,10},{... | collective-permute-start | bytes 1572872 | tf_op jit(solution)/shard_map/ppermute | solution.py:18
  34.4 33.8 %collective-permute-start.2 = (bf16[4,4,64,256]{3,2,1,0:T(8,128)(2,1)S(1)}, bf16[4,4,64,256]{3,2,1,0:T(8,128)(2,1)}, u32[]{:S(2)}, u32[]{:S(2)}) collective-permute-start(bf16[4,4,64,256]{3,2,1,0:T(8,128)(2,1)S(1)} %copy-done.11), channel_id=1, source_target_pairs={{0,12},{4,0},{8,4},{12,8},{1,13},{5,1},{9,5},{13,9},{2,14},{6,2},{... | collective-permute-start | bytes 1572872 | tf_op jit(solution)/shard_map/ppermute | solution.py:20
  69.3 4.4 copy-start.12
  71.7 2.0 copy-start.9
  116.1 1.3 copy-start.6
  164.8 429.2 %reduce-scatter.2.cloned.1.call-start = ((), (), s32[]{:S(2)}) async-start(), calls=%async_computation.5 | async-start | bytes 6291456 | tf_op jit(solution)/shard_map/reduce_scatter | solution.py:92
  195.4 2.0 copy-start.2
  382.0 2.0 copy-start.1
  562.6 5.8 copy-start.5
  568.4 3.5 copy-start.3
  571.9 1.6 copy-start.7
  573.5 3.5 copy-start.10
  580.7 3.4 copy-start.4
  584.1 1.8 copy-start.8
Sparse Core Ops, SparseCore 0:
  10.4 53.7 all-gather.3
  66.3 46.2 all-gather.5
  114.2 44.4 all-gather.7
  164.9 26.2 all-reduce.1
  580.8 13.2 reduce-scatter.1
